TPU v7x, 32 devices: a whole 2x2x4 slice. The times are simulated.
32 devices in a mesh: groups: 2 (over y), seq: 16 (over z, x, core).
Axes of the slice: x: 2, y: 2, z: 4, core: 2. Of those that a mesh axis runs over, the one named last changes fastest.
Arguments:
- qkv: bfloat16 [4096, 32, 384], P(('groups', 'seq')), parts along dimension 0
- routes: int32 [4096, 32], P(('groups', 'seq')), parts along dimension 0, may hold values from 0 to 1, as said below
Outputs:
- attended: bfloat16 [4096, 32, 128], P(('groups', 'seq')), parts along dimension 0
There are 2 independent parts, one for each index of `groups`. A program takes and returns all parts, laid end to end along the dimension named above; each array names one. Nothing has to cross between parts.
Inputs may be any that keep to these rules, and one draw needn't show every extreme that they name: Every cluster of every head holds between 512 and 1536 tokens, and in every head some cluster holds exactly 1536. Numbering the pairs (head h, cluster c) as h * 2 + c, the tokens of one device name each aligned group of 4 pairs exactly 256 times. Integer counts, offsets and slot indices derived from routes may cross between devices packed several to a 32-bit word.
All inputs are finite; a program needn't handle non-finite values.
Results may differ from a plain program's by a relative error of at most 0.0047.
Values may be sent and summed in bfloat16 or wider, within the bound.
No kernel may reach another device: no remote copies, remote signals or barrier semaphores. Data moves between devices by JAX's collectives and lax.ppermute only.
A program may use at most 128 MiB of HBM per device.

v0:
```python
import math
import jax
import jax.numpy as jnp
from jax import lax
from jax.sharding import PartitionSpec as P

CLEN = 1024


def entering(part, axis, combine, identity):
    place = lax.axis_index(axis)
    gathered = lax.all_gather(part, axis)
    state = jnp.zeros_like(part) + jnp.asarray(identity, part.dtype)

    def one(turn, state):
        return combine(state, lax.dynamic_index_in_dim(gathered, turn, 0, False))

    return lax.fori_loop(0, place, one, state)


def attend(queries, keys, values, start, scale):
    block_rows = queries.shape[1]
    span = keys.shape[1]
    scores = jnp.einsum("pqd,pkd->pqk", queries, keys, preferred_element_type=jnp.float32) * scale
    rows = start + jnp.arange(block_rows, dtype=jnp.int32)[:, None]
    cols = jnp.arange(span, dtype=jnp.int32)[None, :]
    scores = jnp.where((cols <= rows)[None], scores, -1e30)
    peak = jnp.max(scores, axis=2, keepdims=True)
    expo = jnp.exp(scores - peak)
    weights = (expo / jnp.sum(expo, axis=2, keepdims=True)).astype(jnp.bfloat16)
    return jnp.einsum("pqk,pkd->pqd", weights, values, preferred_element_type=jnp.float32).astype(
        jnp.bfloat16
    )


def local(qkv, routes):
    tok, heads, width = qkv.shape
    head_size = width // 3
    nseq = lax.axis_size("seq")
    clusters = nseq * tok // CLEN
    pairs_dev = heads * tok // CLEN
    capacity = 3 * CLEN // 2
    block_rows = CLEN // 2
    share = CLEN // nseq
    rows_peer = pairs_dev * share
    total_pairs = heads * clusters
    scale = 1.0 / math.sqrt(head_size)
    member = routes[:, :, None] == jnp.arange(clusters, dtype=jnp.int32)[None, None, :]
    member_flat = member.reshape(tok, total_pairs)
    counts = jnp.sum(member_flat.astype(jnp.int32), axis=0)
    earlier = (jnp.arange(tok)[:, None] > jnp.arange(tok)[None, :]).astype(jnp.bfloat16)
    before = jnp.dot(earlier, member_flat.astype(jnp.bfloat16), preferred_element_type=jnp.float32)
    rank = jnp.sum(jnp.where(member, before.reshape(tok, heads, clusters), 0.0), axis=2).astype(
        jnp.int32
    )
    prefix = entering(counts, "seq", lambda first, second: first + second, jnp.zeros_like(counts))

    def lookup(table):
        return jnp.sum(jnp.where(member, table.reshape(heads, clusters)[None], 0), axis=2)

    group_counts = counts.reshape(total_pairs // pairs_dev, pairs_dev)
    within = (jnp.cumsum(group_counts, axis=1) - group_counts).reshape(total_pairs)
    slot = lookup(prefix) + rank
    pair_index = jnp.arange(heads, dtype=jnp.int32)[None, :] * clusters + routes
    owner = pair_index // pairs_dev
    local_pair = pair_index % pairs_dev
    position = (owner * rows_peer + lookup(within) + rank).reshape(tok * heads)
    target = (local_pair * capacity + slot).reshape(tok * heads)
    outgoing = (
        jnp.zeros((tok * heads, width), jnp.bfloat16)
        .at[position]
        .set(qkv.reshape(tok * heads, width))
    )
    labels = jnp.zeros((tok * heads,), jnp.int32).at[position].set(target)
    arrived, places = (
        lax.all_to_all(outgoing, "seq", split_axis=0, concat_axis=0, tiled=True),
        lax.all_to_all(labels, "seq", split_axis=0, concat_axis=0, tiled=True),
    )
    tiles = jnp.zeros((pairs_dev * capacity, width), jnp.bfloat16).at[places].set(arrived)
    tiles = tiles.reshape(pairs_dev, capacity, width)
    pieces = []
    for index in range(3):
        start = index * block_rows
        stop = start + block_rows
        pieces.append(
            attend(
                tiles[:, start:stop, :head_size],
                tiles[:, :stop, head_size : 2 * head_size],
                tiles[:, :stop, 2 * head_size :],
                start,
                scale,
            )
        )
    results = jnp.concatenate(pieces, axis=1)
    flat_results = results.reshape(pairs_dev * capacity, head_size)
    replies = flat_results[places]
    returned = lax.all_to_all(replies, "seq", split_axis=0, concat_axis=0, tiled=True)
    return returned[position].reshape(tok, heads, head_size)


def solution(mesh):
    placed = (P(("groups", "seq"), None, None), P(("groups", "seq"), None))
    return jax.shard_map(
        local,
        mesh=mesh,
        in_specs=placed,
        out_specs=P(("groups", "seq"), None, None),
        check_vma=False,
    )
```

profile of v0, /device:TPU:11, one launch (start us, length us, event | category | flops | bytes accessed | tf_op | source)
XLA Modules:
  0.0 283.6 jit_solution(1487217478119262765)
XLA Ops:
  0.0 0.8 convert_reduce_fusion
  0.8 0.1 copy.13
  0.9 0.1 reshape.224
  1.0 0.1 reshape.177
  1.1 15.5 %all-gather = s32[16,1,64]{2,1,0:T(1,128)S(1)} all-gather(s32[1,1,64]{2,1,0:T(1,128)S(1)} %reshape.224), channel_id=1, replica_groups=mesh['groups'=2,'seq'=16] {'seq'}, dimensions={0}, use_global_device_ids=true | all-gather | bytes 4352 | tf_op jit(solution)/shard_map/all_gather | solution.py:12
  16.6 0.2 while.10
  16.9 0.1 broadcast_in_dim.100
  17.0 0.1 copy.19
  17.0 0.2 reduce_window_sum.13
  17.2 0.1 reduce_window_sum.14
  17.3 0.1 copy.14
  17.4 0.1 eq.32
  17.5 0.7 eq.27.clone
  18.2 0.1 compare_bitcast_fusion
  18.3 0.9 fusion.30
  19.2 0.8 select_reduce_fusion
  20.0 0.8 fusion.47
  20.8 0.1 copy.17
  20.9 0.1 reshape.178
  21.1 0.1 copy.20
  21.1 0.1 reshape.204
  21.2 16.1 %scatter_custom_fusion = s32[4096]{0:T(1024)} fusion(s32[4096]{0:T(1024)S(1)} %bitcast.33, s32[4096]{0:T(1024)S(1)} %reshape.204, s32[]{:T(128)} %constant.29.clone.1), kind=kCustom, calls=%fused_computation.84 | custom fusion | bytes 16388 | tf_op jit(solution)/shard_map/scatter | solution.py:74
  37.3 9.8 %all-to-all-start = ((s32[16,256,1]{1,2,0:T(1,128)}), s32[16,256,1]{1,2,0:T(1,128)S(1)}, u32[]{:S(2)}, u32[]{:S(2)}) async-start(s32[16,256,1]{1,2,0:T(1,128)} %bitcast.6), calls=%async_computation | async-start | bytes 32768 | tf_op jit(solution)/shard_map/all_to_all | solution.py:77
  47.1 20.5 %scatter_custom_fusion.1 = bf16[4096,384]{1,0:T(8,128)(2,1)} fusion(s32[4096]{0:T(1024)S(1)} %bitcast.34, bf16[4096,384]{1,0:T(8,128)(2,1)} %bitcast.40, bf16[]{:T(256)} %constant.27.clone.1), kind=kCustom, calls=%fused_computation.41 | custom fusion | bytes 3146240 | tf_op jit(solution)/shard_map/scatter | solution.py:72
  67.7 0.0 all-to-all-done
  67.7 6.1 %all-to-all-start.1 = ((bf16[16,256,384]{2,1,0:T(8,128)(2,1)}), bf16[16,256,384]{2,1,0:T(8,128)(2,1)S(1)}, u32[]{:S(2)}, u32[]{:S(2)}) async-start(bf16[16,256,384]{2,1,0:T(8,128)(2,1)} %bitcast.10), calls=%async_computation.1 | async-start | bytes 6291456 | tf_op jit(solution)/shard_map/all_to_all | solution.py:76
  73.8 0.1 iota_compare_fusion.2
  73.8 1.2 iota_compare_fusion.1
  75.0 1.4 iota_compare_fusion
  76.4 67.2 %all-to-all-done.1 = bf16[16,256,384]{2,1,0:T(8,128)(2,1)S(1)} async-done(((bf16[16,256,384]{2,1,0:T(8,128)(2,1)}), bf16[16,256,384]{2,1,0:T(8,128)(2,1)S(1)}, u32[]{:S(2)}, u32[]{:S(2)}) %all-to-all-start.1) | async-done | bytes 3145760 | tf_op jit(solution)/shard_map/all_to_all | solution.py:76
  143.6 21.1 %scatter_custom_fusion.2 = bf16[6144,384]{1,0:T(8,128)(2,1)} fusion(s32[4096]{0:T(1024)S(1)} %bitcast.38, bf16[4096,384]{1,0:T(8,128)(2,1)S(1)} %bitcast.31, bf16[]{:T(256)} %constant.27.clone.1), kind=kCustom, calls=%fused_computation.30 | custom fusion | bytes 4718594 | tf_op jit(solution)/shard_map/scatter | solution.py:79
  164.7 0.0 copy-start
  164.8 8.1 %fusion.21 = f32[4,512,1536]{2,1,0:T(8,128)} fusion(bf16[4,1536,384]{2,1,0:T(8,128)(2,1)} %bitcast.25), kind=kOutput, calls=%fused_computation.38 | convolution fusion | flops 805306368 | bytes 14680064 | tf_op jit(solution)/shard_map/pqd,pkd->pqk/dot_general | solution.py:24
  172.8 0.0 copy-done
  172.8 4.5 %fusion.32 = f32[4,512,1024]{2,1,0:T(8,128)} fusion(bf16[4,1536,384]{2,1,0:T(8,128)(2,1)S(1)} %bitcast.26), kind=kOutput, calls=%fused_computation.49 | convolution fusion | flops 536870912 | bytes 9961472 | tf_op jit(solution)/shard_map/pqd,pkd->pqk/dot_general | solution.py:24
  177.3 0.0 copy-start.2
  177.3 2.8 fusion.37
  180.1 0.0 copy-done.2
  180.1 16.0 %fusion.58 = (f32[4,512]{1,0:T(4,128)S(1)}, f32[4,512,1536]{2,1,0:T(8,128)}) fusion(f32[4,512,1536]{2,1,0:T(8,128)} %fusion.21, pred[512,1536]{1,0:T(8,128)(4,1)S(1)} %copy-done.2), kind=kOutput, calls=%fused_computation.95 | output fusion | flops 18875904 | bytes 25960448 | tf_op jit(solution)/shard_map/sub | solution.py:29
  196.1 0.0 copy-start.3
  196.1 6.6 %fusion.27 = bf16[4,512,128]{2,1,0:T(8,128)(2,1)S(1)} fusion(bf16[4,1536,384]{2,1,0:T(8,128)(2,1)S(1)} %bitcast.28, f32[4,512,1536]{2,1,0:T(8,128)} %get-tuple-element.42, f32[4,512]{1,0:T(4,128)S(1)} %get-tuple-element.41), kind=kOutput, calls=%fused_computation.45 | convolution fusion | flops 811859968 | bytes 14688256 | tf_op jit(solution)/shard_map/pqk,pkd->pqd/dot_general | solution.py:31
  202.6 0.0 copy-done.3
  202.6 13.0 %fusion.59 = (f32[4,512]{1,0:T(4,128)S(1)}, f32[4,512,1024]{2,1,0:T(8,128)}) fusion(f32[4,512,1024]{2,1,0:T(8,128)} %fusion.32, pred[512,1024]{1,0:T(8,128)(4,1)S(1)} %copy-done.3), kind=kOutput, calls=%fused_computation.96 | output fusion | flops 12583935 | bytes 17309696 | tf_op jit(solution)/shard_map/sub | solution.py:29
  215.6 0.0 copy-start.1
  215.6 4.9 %fusion.25 = bf16[4,512,128]{2,1,0:T(8,128)(2,1)S(1)} fusion(f32[4,512,1024]{2,1,0:T(8,128)} %get-tuple-element.44, f32[4,512]{1,0:T(4,128)S(1)} %get-tuple-element.43, bf16[4,1536,384]{2,1,0:T(8,128)(2,1)S(1)} %bitcast.29), kind=kOutput, calls=%fused_computation.43 | convolution fusion | flops 541327360 | bytes 9969664 | tf_op jit(solution)/shard_map/pqk,pkd->pqd/dot_general | solution.py:31
  220.5 0.0 copy-done.1
  220.5 2.1 fusion.60
  222.7 1.0 fusion.26
  223.6 0.1 pad_maximum_fusion
  223.7 15.0 %gather_fusion = bf16[4096,128]{1,0:T(8,128)(2,1)} fusion(bf16[6144,128]{1,0:T(8,128)(2,1)S(1)} %bitcast.24, s32[4096]{0:T(1024)S(1)} %broadcast_clamp_fusion.1), kind=kCustom, calls=%fused_computation | custom fusion | bytes 2113536 | tf_op jit(solution)/shard_map/gather | solution.py:96
  238.8 4.9 %all-to-all-start.2 = ((bf16[16,256,128]{2,1,0:T(8,128)(2,1)}), bf16[16,256,128]{2,1,0:T(8,128)(2,1)S(1)}, u32[]{:S(2)}, u32[]{:S(2)}) async-start(bf16[16,256,128]{2,1,0:T(8,128)(2,1)} %bitcast.14), calls=%async_computation.2 | async-start | bytes 2097152 | tf_op jit(solution)/shard_map/all_to_all | solution.py:97
  243.7 24.9 %all-to-all-done.2 = bf16[16,256,128]{2,1,0:T(8,128)(2,1)S(1)} async-done(((bf16[16,256,128]{2,1,0:T(8,128)(2,1)}), bf16[16,256,128]{2,1,0:T(8,128)(2,1)S(1)}, u32[]{:S(2)}, u32[]{:S(2)}) %all-to-all-start.2) | async-done | bytes 1048608 | tf_op jit(solution)/shard_map/all_to_all | solution.py:97
  268.5 15.0 %gather_fusion.1 = bf16[4096,128]{1,0:T(8,128)(2,1)} fusion(bf16[4096,128]{1,0:T(8,128)(2,1)S(1)} %bitcast.23, s32[4096]{0:T(1024)S(1)} %broadcast_clamp_fusion), kind=kCustom, calls=%fused_computation.1 | custom fusion | bytes 2113536 | tf_op jit(solution)/shard_map/gather | solution.py:98
  (18 shorter events, 0.2 us)
Async XLA Ops:
  37.3 30.3 %all-to-all-start = ((s32[16,256,1]{1,2,0:T(1,128)}), s32[16,256,1]{1,2,0:T(1,128)S(1)}, u32[]{:S(2)}, u32[]{:S(2)}) async-start(s32[16,256,1]{1,2,0:T(1,128)} %bitcast.6), calls=%async_computation | async-start | bytes 32768 | tf_op jit(solution)/shard_map/all_to_all | solution.py:77
  67.7 76.0 %all-to-all-start.1 = ((bf16[16,256,384]{2,1,0:T(8,128)(2,1)}), bf16[16,256,384]{2,1,0:T(8,128)(2,1)S(1)}, u32[]{:S(2)}, u32[]{:S(2)}) async-start(bf16[16,256,384]{2,1,0:T(8,128)(2,1)} %bitcast.10), calls=%async_computation.1 | async-start | bytes 6291456 | tf_op jit(solution)/shard_map/all_to_all | solution.py:76
  164.7 8.1 %copy-start = (bf16[6144,384]{1,0:T(8,128)(2,1)S(1)}, bf16[6144,384]{1,0:T(8,128)(2,1)}, u32[]{:S(2)}) copy-start(bf16[6144,384]{1,0:T(8,128)(2,1)} %scatter_custom_fusion.2) | copy-start | bytes 14155780
  177.3 2.8 copy-start.2
  196.1 6.6 %copy-start.3 = (pred[512,1024]{1,0:T(8,128)(4,1)S(1)}, pred[512,1024]{1,0:T(8,128)(4,1)}, u32[]{:S(2)}) copy-start(pred[512,1024]{1,0:T(8,128)(4,1)} %iota_compare_fusion.1) | copy-start | bytes 1572868
  215.6 4.9 %copy-start.1 = (f32[4,512,512]{1,2,0:T(8,128)S(1)}, f32[4,512,512]{1,2,0:T(8,128)}, u32[]{:S(2)}) copy-start(f32[4,512,512]{1,2,0:T(8,128)} %fusion.37) | copy-start | bytes 12582916
  238.8 29.8 %all-to-all-start.2 = ((bf16[16,256,128]{2,1,0:T(8,128)(2,1)}), bf16[16,256,128]{2,1,0:T(8,128)(2,1)S(1)}, u32[]{:S(2)}, u32[]{:S(2)}) async-start(bf16[16,256,128]{2,1,0:T(8,128)(2,1)} %bitcast.14), calls=%async_computation.2 | async-start | bytes 2097152 | tf_op jit(solution)/shard_map/all_to_all | solution.py:97
where the time goes:
time: 284 us
  waiting for transfers between devices  92.1 us (32%)
  local copies, waits for them, and re-layouts  89.7 us (32%)
  other arithmetic  36.7 us (13%)
  matrix products  28.6 us (10%)
  starting transfers between devices  20.8 us (7%)
  blocking collectives  15.5 us (5%)
    all_to_all x1, waiting for transfers between devices, local(): lax.all_to_all(outgoing, 'seq', split_axis=0, concat_axis=0, tiled=True)  67.2 us
    sub x3, other arithmetic, attend(): expo = jnp.exp(scores - peak)  31.1 us
    all_to_all x1, waiting for transfers between devices, local(): lax.all_to_all(replies, 'seq', split_axis=0, concat_axis=0, tiled=True)  24.9 us
    scatter x1, local copies, waits for them, and re-layouts, local(): jnp.zeros((pairs_dev * capacity, width), jnp.bfloat16).at[places]  21.1 us
    scatter x1, local copies, waits for them, and re-layouts, local(): outgoing = jnp.zeros((tok * heads, width), jnp.bfloat16).at[position].set...  20.5 us
    scatter x1, local copies, waits for them, and re-layouts, local(): labels = jnp.zeros((tok * heads,), jnp.int32).at[position].set(target)  16.1 us
    all_gather x1, blocking collectives, entering(): gathered = lax.all_gather(part, axis)  15.5 us
    dot_general x3, matrix products, attend(): jnp.einsum('pqd,pkd->pqk', queries, keys, preferred_element_type=jnp.floa...  15.3 us
  transfers between devices with their start and end apart: 3, of which 2 were waited for; matrix products, arithmetic and copies ran while one was open for 8% of the time, Pallas kernels for 0%

commit v1 on v0

--- a/solution.py
+++ b/solution.py
@@ -5,6 +5,28 @@
 from jax.sharding import PartitionSpec as P
 
 CLEN = 1024
+
+
+def in_blocks(value, dim, size):
+    before, after = (value.shape[:dim], value.shape[dim + 1 :])
+    return jnp.moveaxis(value.reshape(*before, size, -1, *after), dim, 0)
+
+
+def joined_along(pieces, dim):
+    dims = list(pieces.shape[1:])
+    dims[dim] *= pieces.shape[0]
+    return jnp.moveaxis(pieces, 0, dim).reshape(dims)
+
+
+def exchange_in_pairs(array, axis, split_dim, concat_dim):
+    peers, index = (lax.axis_size(axis), lax.axis_index(axis))
+    tiles = in_blocks(array, split_dim, peers)
+    outs = [tiles[index]]
+    for step in range(1, peers):
+        sent = tiles[index ^ step]
+        outs.append(lax.ppermute(sent, axis, [(i, i ^ step) for i in range(peers)]))
+    tiles = jnp.stack(outs)[index ^ jnp.arange(peers)]
+    return joined_along(tiles, concat_dim)
 
 
 def entering(part, axis, combine, identity):
@@ -94,7 +116,7 @@
     results = jnp.concatenate(pieces, axis=1)
     flat_results = results.reshape(pairs_dev * capacity, head_size)
     replies = flat_results[places]
-    returned = lax.all_to_all(replies, "seq", split_axis=0, concat_axis=0, tiled=True)
+    returned = exchange_in_pairs(replies, "seq", 0, 0)
     return returned[position].reshape(tok, heads, head_size)
 
 

time: 284 us -> 289 us (1.018)
  waiting for transfers between devices: 92.1 us -> 74.3 us
  starting transfers between devices: 20.8 us -> 33 us
  local copies, waits for them, and re-layouts: 89.7 us -> 99.2 us
    all_to_all x1 -> x0, waiting for transfers between devices: 24.9 us -> none  [local(): lax.all_to_all(replies, 'seq', split_axis=0, concat_axis=0, tiled=True)]
    ppermute x0 -> x15, starting transfers between devices: none -> 17.1 us  [exchange_in_pairs(): outs.append(lax.ppermute(sent, axis, [(i, i ^ step) for i in range(peers)]))]
    unnamed x9 -> x23, local copies, waits for them, and re-layouts: 0.12 us -> 9 us
    ppermute x0 -> x15, waiting for transfers between devices: none -> 7.09 us  [exchange_in_pairs(): outs.append(lax.ppermute(sent, axis, [(i, i ^ step) for i in range(peers)]))]
    all_to_all x1 -> x0, starting transfers between devices: 4.9 us -> none  [local(): lax.all_to_all(replies, 'seq', split_axis=0, concat_axis=0, tiled=True)]
    gather x1, local copies, waits for them, and re-layouts: 15 us -> 12.1 us  [local(): replies = flat_results[places]]
  transfers between devices with their start and end apart: 3 -> 17, of which waited for: 2 -> 5; matrix products, arithmetic and copies ran while one was open for 8% -> 11% of each run, Pallas kernels for 0% -> 0%
where the time goes in v1:
time: 289 us; the launch traced here: 288 us
  local copies, waits for them, and re-layouts  99.2 us (34%)
  waiting for transfers between devices  74.3 us (26%)
  other arithmetic  36.8 us (13%)
  starting transfers between devices  33 us (11%)
  matrix products  28.6 us (10%)
  blocking collectives  15.5 us (5%)
    all_to_all x1, waiting for transfers between devices, local(): lax.all_to_all(outgoing, 'seq', split_axis=0, concat_axis=0, tiled=True)  67.2 us
    sub x3, other arithmetic, attend(): expo = jnp.exp(scores - peak)  31.2 us
    scatter x1, local copies, waits for them, and re-layouts, local(): jnp.zeros((pairs_dev * capacity, width), jnp.bfloat16).at[places]  21.1 us
    scatter x1, local copies, waits for them, and re-layouts, local(): outgoing = jnp.zeros((tok * heads, width), jnp.bfloat16).at[position].set...  20.5 us
    ppermute x15, starting transfers between devices, exchange_in_pairs(): outs.append(lax.ppermute(sent, axis, [(i, i ^ step) for i in range(peers)]))  17.1 us
    scatter x1, local copies, waits for them, and re-layouts, local(): labels = jnp.zeros((tok * heads,), jnp.int32).at[position].set(target)  16.1 us
    all_gather x1, blocking collectives, entering(): gathered = lax.all_gather(part, axis)  15.5 us
    dot_general x3, matrix products, attend(): jnp.einsum('pqd,pkd->pqk', queries, keys, preferred_element_type=jnp.floa...  15.3 us
  transfers between devices with their start and end apart: 17, of which 5 were waited for; matrix products, arithmetic and copies ran while one was open for 11% of the time, Pallas kernels for 0%

profile of v1, /device:TPU:11, one launch (start us, length us, event | category | flops | bytes accessed | tf_op | source)
XLA Modules:
  0.0 287.6 jit_solution(1948455184724495809)
XLA Ops:
  0.0 0.8 convert_reduce_fusion
  0.9 0.1 reshape.254
  1.1 15.5 %all-gather = s32[16,1,64]{2,1,0:T(1,128)S(1)} all-gather(s32[1,1,64]{2,1,0:T(1,128)S(1)} %reshape.254), channel_id=1, replica_groups=mesh['groups'=2,'seq'=16] {'seq'}, dimensions={0}, use_global_device_ids=true | all-gather | bytes 4352 | tf_op jit(solution)/shard_map/all_gather | solution.py:34
  16.6 0.2 while.10
  17.0 0.2 reduce_window_sum.13
  17.4 0.1 eq.32
  17.5 0.7 eq.27.clone
  18.3 0.9 fusion.30
  19.2 0.8 select_reduce_fusion
  20.0 0.8 fusion.47
  20.8 0.1 copy.17
  20.9 0.1 reshape.198
  21.2 16.1 %scatter_custom_fusion = s32[4096]{0:T(1024)} fusion(s32[4096]{0:T(1024)S(1)} %bitcast.96, s32[4096]{0:T(1024)S(1)} %reshape.234, s32[]{:T(128)} %constant.37.clone.1), kind=kCustom, calls=%fused_computation.116 | custom fusion | bytes 16388 | tf_op jit(solution)/shard_map/scatter | solution.py:96
  37.3 9.8 %all-to-all-start = ((s32[16,256,1]{1,2,0:T(1,128)}), s32[16,256,1]{1,2,0:T(1,128)S(1)}, u32[]{:S(2)}, u32[]{:S(2)}) async-start(s32[16,256,1]{1,2,0:T(1,128)} %bitcast.6), calls=%async_computation | async-start | bytes 32768 | tf_op jit(solution)/shard_map/all_to_all | solution.py:99
  47.1 20.5 %scatter_custom_fusion.1 = bf16[4096,384]{1,0:T(8,128)(2,1)} fusion(s32[4096]{0:T(1024)S(1)} %bitcast.97, bf16[4096,384]{1,0:T(8,128)(2,1)} %bitcast.103, bf16[]{:T(256)} %constant.36.clone.1), kind=kCustom, calls=%fused_computation.42 | custom fusion | bytes 3146240 | tf_op jit(solution)/shard_map/scatter | solution.py:94
  67.7 6.1 %all-to-all-start.1 = ((bf16[16,256,384]{2,1,0:T(8,128)(2,1)}), bf16[16,256,384]{2,1,0:T(8,128)(2,1)S(1)}, u32[]{:S(2)}, u32[]{:S(2)}) async-start(bf16[16,256,384]{2,1,0:T(8,128)(2,1)} %bitcast.10), calls=%async_computation.1 | async-start | bytes 6291456 | tf_op jit(solution)/shard_map/all_to_all | solution.py:98
  73.9 1.2 iota_compare_fusion.1
  75.0 1.4 iota_compare_fusion
  76.5 67.2 %all-to-all-done.1 = bf16[16,256,384]{2,1,0:T(8,128)(2,1)S(1)} async-done(((bf16[16,256,384]{2,1,0:T(8,128)(2,1)}), bf16[16,256,384]{2,1,0:T(8,128)(2,1)S(1)}, u32[]{:S(2)}, u32[]{:S(2)}) %all-to-all-start.1) | async-done | bytes 3145760 | tf_op jit(solution)/shard_map/all_to_all | solution.py:98
  143.6 21.1 %scatter_custom_fusion.2 = bf16[6144,384]{1,0:T(8,128)(2,1)} fusion(s32[4096]{0:T(1024)S(1)} %bitcast.101, bf16[4096,384]{1,0:T(8,128)(2,1)S(1)} %bitcast.94, bf16[]{:T(256)} %constant.36.clone.1), kind=kCustom, calls=%fused_computation.31 | custom fusion | bytes 4718594 | tf_op jit(solution)/shard_map/scatter | solution.py:101
  164.8 8.1 %fusion.21 = f32[4,512,1536]{2,1,0:T(8,128)} fusion(bf16[4,1536,384]{2,1,0:T(8,128)(2,1)} %bitcast.87), kind=kOutput, calls=%fused_computation.39 | convolution fusion | flops 805306368 | bytes 14680064 | tf_op jit(solution)/shard_map/pqd,pkd->pqk/dot_general | solution.py:46
  172.8 4.5 %fusion.32 = f32[4,512,1024]{2,1,0:T(8,128)} fusion(bf16[4,1536,384]{2,1,0:T(8,128)(2,1)S(1)} %bitcast.88), kind=kOutput, calls=%fused_computation.50 | convolution fusion | flops 536870912 | bytes 9961472 | tf_op jit(solution)/shard_map/pqd,pkd->pqk/dot_general | solution.py:46
  177.3 2.8 fusion.37
  180.1 16.1 %fusion.59 = (f32[4,512]{1,0:T(4,128)S(1)}, f32[4,512,1536]{2,1,0:T(8,128)}) fusion(f32[4,512,1536]{2,1,0:T(8,128)} %fusion.21, pred[512,1536]{1,0:T(8,128)(4,1)S(1)} %copy-done.2), kind=kOutput, calls=%fused_computation.130 | output fusion | flops 18875904 | bytes 25960448 | tf_op jit(solution)/shard_map/sub | solution.py:51
  196.1 6.6 %fusion.27 = bf16[4,512,128]{2,1,0:T(8,128)(2,1)S(1)} fusion(bf16[4,1536,384]{2,1,0:T(8,128)(2,1)S(1)} %bitcast.90, f32[4,512,1536]{2,1,0:T(8,128)} %get-tuple-element.58, f32[4,512]{1,0:T(4,128)S(1)} %get-tuple-element.57), kind=kOutput, calls=%fused_computation.46 | convolution fusion | flops 811859968 | bytes 14688256 | tf_op jit(solution)/shard_map/pqk,pkd->pqd/dot_general | solution.py:53
  202.7 13.0 %fusion.60 = (f32[4,512]{1,0:T(4,128)S(1)}, f32[4,512,1024]{2,1,0:T(8,128)}) fusion(f32[4,512,1024]{2,1,0:T(8,128)} %fusion.32, pred[512,1024]{1,0:T(8,128)(4,1)S(1)} %copy-done.3), kind=kOutput, calls=%fused_computation.131 | output fusion | flops 12583935 | bytes 17309696 | tf_op jit(solution)/shard_map/sub | solution.py:51
  215.7 4.9 %fusion.25 = bf16[4,512,128]{2,1,0:T(8,128)(2,1)S(1)} fusion(f32[4,512,1024]{2,1,0:T(8,128)} %get-tuple-element.60, f32[4,512]{1,0:T(4,128)S(1)} %get-tuple-element.59, bf16[4,1536,384]{2,1,0:T(8,128)(2,1)S(1)} %bitcast.91), kind=kOutput, calls=%fused_computation.44 | convolution fusion | flops 541327360 | bytes 9969664 | tf_op jit(solution)/shard_map/pqk,pkd->pqd/dot_general | solution.py:53
  220.6 2.1 fusion.61
  222.7 1.0 fusion.26
  223.7 0.1 pad_maximum_fusion
  223.8 12.1 %gather_fusion = bf16[4096,128]{1,0:T(8,128)(2,1)S(1)} fusion(bf16[6144,128]{1,0:T(8,128)(2,1)S(1)} %bitcast.86, s32[4096]{0:T(1024)S(1)} %broadcast_clamp_fusion.1), kind=kCustom, calls=%fused_computation | custom fusion | bytes 2113536 | tf_op jit(solution)/shard_map/gather | solution.py:118
  235.9 0.9 dynamic-slice_bitcast_fusion
  236.9 0.2 collective-permute-start
  237.1 1.9 collective-permute-start.2
  239.0 1.6 collective-permute-start.4
  240.6 0.6 bitcast_dynamic-update-slice_fusion.14
  241.2 2.8 collective-permute-start.6
  244.0 0.6 bitcast_dynamic-update-slice_fusion.13
  244.7 1.1 collective-permute-start.7
  245.8 0.6 bitcast_dynamic-update-slice_fusion.12
  246.4 1.3 collective-permute-start.8
  247.8 0.6 bitcast_dynamic-update-slice_fusion.11
  248.4 1.1 collective-permute-start.9
  249.5 0.6 bitcast_dynamic-update-slice_fusion.10
  250.1 2.7 collective-permute-start.10
  252.8 0.6 bitcast_dynamic-update-slice_fusion.9
  253.4 0.6 bitcast_dynamic-update-slice_fusion.8
  254.1 1.6 collective-permute-start.12
  255.6 0.6 bitcast_dynamic-update-slice_fusion.7
  256.3 1.6 collective-permute-start.13
  257.8 0.6 bitcast_dynamic-update-slice_fusion.6
  258.5 1.3 collective-permute-start.14
  259.7 0.6 bitcast_dynamic-update-slice_fusion.5
  260.4 0.6 bitcast_dynamic-update-slice_fusion.4
  261.0 2.9 %collective-permute-done.11 = bf16[256,128]{1,0:T(8,128)(2,1)S(1)} collective-permute-done((bf16[256,128]{1,0:T(8,128)(2,1)S(1)}, bf16[256,128]{1,0:T(8,128)(2,1)S(1)}, u32[]{:S(2)}, u32[]{:S(2)}) %collective-permute-start.11) | collective-permute-done | bytes 65568 | tf_op jit(solution)/shard_map/ppermute | solution.py:27
  263.9 0.6 bitcast_dynamic-update-slice_fusion.3
  264.5 0.8 collective-permute-done.12
  265.3 0.6 bitcast_dynamic-update-slice_fusion.2
  265.9 2.6 collective-permute-done.13
  268.6 0.6 bitcast_dynamic-update-slice_fusion.1
  269.2 0.8 collective-permute-done.14
  270.0 0.6 bitcast_dynamic-update-slice_fusion
  270.6 2.0 gather_fusion.1
  272.6 15.0 %gather_fusion.2 = bf16[4096,128]{1,0:T(8,128)(2,1)} fusion(bf16[4096,128]{1,0:T(8,128)(2,1)S(1)} %bitcast.85, s32[4096]{0:T(1024)S(1)} %broadcast_clamp_fusion), kind=kCustom, calls=%fused_computation.2 | custom fusion | bytes 2113536 | tf_op jit(solution)/shard_map/gather | solution.py:120
  (54 shorter events, 1.1 us)
Async XLA Ops:
  37.3 30.3 %all-to-all-start = ((s32[16,256,1]{1,2,0:T(1,128)}), s32[16,256,1]{1,2,0:T(1,128)S(1)}, u32[]{:S(2)}, u32[]{:S(2)}) async-start(s32[16,256,1]{1,2,0:T(1,128)} %bitcast.6), calls=%async_computation | async-start | bytes 32768 | tf_op jit(solution)/shard_map/all_to_all | solution.py:99
  67.7 76.0 %all-to-all-start.1 = ((bf16[16,256,384]{2,1,0:T(8,128)(2,1)}), bf16[16,256,384]{2,1,0:T(8,128)(2,1)S(1)}, u32[]{:S(2)}, u32[]{:S(2)}) async-start(bf16[16,256,384]{2,1,0:T(8,128)(2,1)} %bitcast.10), calls=%async_computation.1 | async-start | bytes 6291456 | tf_op jit(solution)/shard_map/all_to_all | solution.py:98
  164.8 8.1 %copy-start = (bf16[6144,384]{1,0:T(8,128)(2,1)S(1)}, bf16[6144,384]{1,0:T(8,128)(2,1)}, u32[]{:S(2)}) copy-start(bf16[6144,384]{1,0:T(8,128)(2,1)} %scatter_custom_fusion.2) | copy-start | bytes 14155780
  177.3 2.8 copy-start.2
  196.1 6.6 %copy-start.3 = (pred[512,1024]{1,0:T(8,128)(4,1)S(1)}, pred[512,1024]{1,0:T(8,128)(4,1)}, u32[]{:S(2)}) copy-start(pred[512,1024]{1,0:T(8,128)(4,1)} %iota_compare_fusion.1) | copy-start | bytes 1572868
  215.7 4.9 %copy-start.1 = (f32[4,512,512]{1,2,0:T(8,128)S(1)}, f32[4,512,512]{1,2,0:T(8,128)}, u32[]{:S(2)}) copy-start(f32[4,512,512]{1,2,0:T(8,128)} %fusion.37) | copy-start | bytes 12582916
  236.9 3.7 %collective-permute-start = (bf16[256,128]{1,0:T(8,128)(2,1)S(1)}, bf16[256,128]{1,0:T(8,128)(2,1)S(1)}, u32[]{:S(2)}, u32[]{:S(2)}) collective-permute-start(bf16[256,128]{1,0:T(8,128)(2,1)S(1)} %get-tuple-element.53), channel_id=1, source_target_pairs={{0,1},{1,0},{2,3},{3,2},{4,5},{5,4},{6,7},{7,6},{8,9},{9,8},{10,11... | collective-permute-start | bytes 196616 | tf_op jit(solution)/shard_map/ppermute | solution.py:27
  237.1 4.1 %collective-permute-start.1 = (bf16[256,128]{1,0:T(8,128)(2,1)S(1)}, bf16[256,128]{1,0:T(8,128)(2,1)S(1)}, u32[]{:S(2)}, u32[]{:S(2)}) collective-permute-start(bf16[256,128]{1,0:T(8,128)(2,1)S(1)} %get-tuple-element.52), channel_id=1, source_target_pairs={{0,2},{1,3},{2,0},{3,1},{4,6},{5,7},{6,4},{7,5},{8,10},{9,11},{10,... | collective-permute-start | bytes 196616 | tf_op jit(solution)/shard_map/ppermute | solution.py:27
  237.1 7.6 %collective-permute-start.2 = (bf16[256,128]{1,0:T(8,128)(2,1)S(1)}, bf16[256,128]{1,0:T(8,128)(2,1)S(1)}, u32[]{:S(2)}, u32[]{:S(2)}) collective-permute-start(bf16[256,128]{1,0:T(8,128)(2,1)S(1)} %get-tuple-element.51), channel_id=1, source_target_pairs={{0,3},{1,2},{2,1},{3,0},{4,7},{5,6},{6,5},{7,4},{8,11},{9,10},{10,... | collective-permute-start | bytes 196616 | tf_op jit(solution)/shard_map/ppermute | solution.py:27
  239.0 7.4 %collective-permute-start.3 = (bf16[256,128]{1,0:T(8,128)(2,1)S(1)}, bf16[256,128]{1,0:T(8,128)(2,1)S(1)}, u32[]{:S(2)}, u32[]{:S(2)}) collective-permute-start(bf16[256,128]{1,0:T(8,128)(2,1)S(1)} %get-tuple-element.50), channel_id=1, source_target_pairs={{0,4},{1,5},{2,6},{3,7},{4,0},{5,1},{6,2},{7,3},{8,12},{9,13},{10,... | collective-permute-start | bytes 196616 | tf_op jit(solution)/shard_map/ppermute | solution.py:27
  239.0 9.4 %collective-permute-start.4 = (bf16[256,128]{1,0:T(8,128)(2,1)S(1)}, bf16[256,128]{1,0:T(8,128)(2,1)S(1)}, u32[]{:S(2)}, u32[]{:S(2)}) collective-permute-start(bf16[256,128]{1,0:T(8,128)(2,1)S(1)} %get-tuple-element.49), channel_id=1, source_target_pairs={{0,5},{1,4},{2,7},{3,6},{4,1},{5,0},{6,3},{7,2},{8,13},{9,12},{10,... | collective-permute-start | bytes 196616 | tf_op jit(solution)/shard_map/ppermute | solution.py:27
  240.6 9.5 %collective-permute-start.5 = (bf16[256,128]{1,0:T(8,128)(2,1)S(1)}, bf16[256,128]{1,0:T(8,128)(2,1)S(1)}, u32[]{:S(2)}, u32[]{:S(2)}) collective-permute-start(bf16[256,128]{1,0:T(8,128)(2,1)S(1)} %get-tuple-element.48), channel_id=1, source_target_pairs={{0,6},{1,7},{2,4},{3,5},{4,2},{5,3},{6,0},{7,1},{8,14},{9,15},{10,... | collective-permute-start | bytes 196616 | tf_op jit(solution)/shard_map/ppermute | solution.py:27
  241.2 12.2 %collective-permute-start.6 = (bf16[256,128]{1,0:T(8,128)(2,1)S(1)}, bf16[256,128]{1,0:T(8,128)(2,1)S(1)}, u32[]{:S(2)}, u32[]{:S(2)}) collective-permute-start(bf16[256,128]{1,0:T(8,128)(2,1)S(1)} %get-tuple-element.47), channel_id=1, source_target_pairs={{0,7},{1,6},{2,5},{3,4},{4,3},{5,2},{6,1},{7,0},{8,15},{9,14},{10,... | collective-permute-start | bytes 196616 | tf_op jit(solution)/shard_map/ppermute | solution.py:27
  244.7 9.4 %collective-permute-start.7 = (bf16[256,128]{1,0:T(8,128)(2,1)S(1)}, bf16[256,128]{1,0:T(8,128)(2,1)S(1)}, u32[]{:S(2)}, u32[]{:S(2)}) collective-permute-start(bf16[256,128]{1,0:T(8,128)(2,1)S(1)} %get-tuple-element.46), channel_id=1, source_target_pairs={{0,8},{1,9},{2,10},{3,11},{4,12},{5,13},{6,14},{7,15},{8,0},{9,1},... | collective-permute-start | bytes 196616 | tf_op jit(solution)/shard_map/ppermute | solution.py:27
  246.4 9.8 %collective-permute-start.8 = (bf16[256,128]{1,0:T(8,128)(2,1)S(1)}, bf16[256,128]{1,0:T(8,128)(2,1)S(1)}, u32[]{:S(2)}, u32[]{:S(2)}) collective-permute-start(bf16[256,128]{1,0:T(8,128)(2,1)S(1)} %get-tuple-element.45), channel_id=1, source_target_pairs={{0,9},{1,8},{2,11},{3,10},{4,13},{5,12},{6,15},{7,14},{8,1},{9,0},... | collective-permute-start | bytes 196616 | tf_op jit(solution)/shard_map/ppermute | solution.py:27
  248.4 10.1 %collective-permute-start.9 = (bf16[256,128]{1,0:T(8,128)(2,1)S(1)}, bf16[256,128]{1,0:T(8,128)(2,1)S(1)}, u32[]{:S(2)}, u32[]{:S(2)}) collective-permute-start(bf16[256,128]{1,0:T(8,128)(2,1)S(1)} %get-tuple-element.44), channel_id=1, source_target_pairs={{0,10},{1,11},{2,8},{3,9},{4,14},{5,15},{6,12},{7,13},{8,2},{9,3},... | collective-permute-start | bytes 196616 | tf_op jit(solution)/shard_map/ppermute | solution.py:27
  250.1 10.3 %collective-permute-start.10 = (bf16[256,128]{1,0:T(8,128)(2,1)S(1)}, bf16[256,128]{1,0:T(8,128)(2,1)S(1)}, u32[]{:S(2)}, u32[]{:S(2)}) collective-permute-start(bf16[256,128]{1,0:T(8,128)(2,1)S(1)} %get-tuple-element.43), channel_id=1, source_target_pairs={{0,11},{1,10},{2,9},{3,8},{4,15},{5,14},{6,13},{7,12},{8,3},{9,2},... | collective-permute-start | bytes 196616 | tf_op jit(solution)/shard_map/ppermute | solution.py:27
  253.4 10.5 %collective-permute-start.11 = (bf16[256,128]{1,0:T(8,128)(2,1)S(1)}, bf16[256,128]{1,0:T(8,128)(2,1)S(1)}, u32[]{:S(2)}, u32[]{:S(2)}) collective-permute-start(bf16[256,128]{1,0:T(8,128)(2,1)S(1)} %get-tuple-element.42), channel_id=1, source_target_pairs={{0,12},{1,13},{2,14},{3,15},{4,8},{5,9},{6,10},{7,11},{8,4},{9,5},... | collective-permute-start | bytes 196616 | tf_op jit(solution)/shard_map/ppermute | solution.py:27
  254.1 11.2 %collective-permute-start.12 = (bf16[256,128]{1,0:T(8,128)(2,1)S(1)}, bf16[256,128]{1,0:T(8,128)(2,1)S(1)}, u32[]{:S(2)}, u32[]{:S(2)}) collective-permute-start(bf16[256,128]{1,0:T(8,128)(2,1)S(1)} %get-tuple-element.41), channel_id=1, source_target_pairs={{0,13},{1,12},{2,15},{3,14},{4,9},{5,8},{6,11},{7,10},{8,5},{9,4},... | collective-permute-start | bytes 196616 | tf_op jit(solution)/shard_map/ppermute | solution.py:27
  256.3 12.3 %collective-permute-start.13 = (bf16[256,128]{1,0:T(8,128)(2,1)S(1)}, bf16[256,128]{1,0:T(8,128)(2,1)S(1)}, u32[]{:S(2)}, u32[]{:S(2)}) collective-permute-start(bf16[256,128]{1,0:T(8,128)(2,1)S(1)} %get-tuple-element.40), channel_id=1, source_target_pairs={{0,14},{1,15},{2,12},{3,13},{4,10},{5,11},{6,8},{7,9},{8,6},{9,7},... | collective-permute-start | bytes 196616 | tf_op jit(solution)/shard_map/ppermute | solution.py:27
  258.5 11.5 %collective-permute-start.14 = (bf16[256,128]{1,0:T(8,128)(2,1)S(1)}, bf16[256,128]{1,0:T(8,128)(2,1)S(1)}, u32[]{:S(2)}, u32[]{:S(2)}) collective-permute-start(bf16[256,128]{1,0:T(8,128)(2,1)S(1)} %get-tuple-element.39), channel_id=1, source_target_pairs={{0,15},{1,14},{2,13},{3,12},{4,11},{5,10},{6,9},{7,8},{8,7},{9,6},... | collective-permute-start | bytes 196616 | tf_op jit(solution)/shard_map/ppermute | solution.py:27
